TPU v7x, 32 devices: a whole 2x2x4 slice. The times are simulated.
32 devices in a mesh: dp: 16 (over z, x, core), fsdp: 2 (over y).
Axes of the slice: x: 2, y: 2, z: 4, core: 2. Of those that a mesh axis runs over, the one named last changes fastest.
Arguments:
- inputs: bfloat16 [128, 256, 512], P(('dp', 'fsdp')), may hold values from -0.3125 to 0.3125
- out_grad: bfloat16 [128, 256, 512], P(('dp', 'fsdp')), may hold values from -6 to 6
- coeff_fixed: int32 [128, 16], P(('dp', 'fsdp')), may hold values from 0 to 4096
- atom_counts: int32 [128], P(('dp', 'fsdp')), may hold values from 64 to 256, as said below
- experts: bfloat16 [16, 512, 512], P(None, ('dp', 'fsdp')), may hold values from -0.125 to 0.125
Outputs:
- in_grad: bfloat16 [128, 256, 512], P(('dp', 'fsdp'))
- expert_grad: float32 [16, 512, 512], P(None, ('dp', 'fsdp'))
Inputs may be any that keep to these rules, and one draw needn't show every extreme that they name: `atom_counts`: some system has exactly 256 atoms and some exactly 64.
All inputs are finite; a program needn't handle non-finite values.
Results may differ from a plain program's by a relative error of at most 0.0049.
Values may be sent and summed in bfloat16 or wider, within the bound.
A program may use at most 128 MiB of HBM per device.

v0:
```python
import jax
import jax.numpy as jnp
from jax import lax
from jax.sharding import PartitionSpec as P

HIGH = lax.Precision.HIGHEST


def shards(inputs, out_grad, coeff_fixed, atom_counts, experts):
    n_sys, n_slots, width = inputs.shape
    n_exp = experts.shape[0]
    coeffs = coeff_fixed.astype(jnp.float32) / 4096.0
    valid = lax.broadcasted_iota(jnp.int32, (n_sys, n_slots), 1) < atom_counts[:, None]
    masked = jnp.where(valid[:, :, None], out_grad, jnp.zeros_like(out_grad))
    whole = lax.all_gather(experts, ("dp", "fsdp"), axis=1, tiled=True)
    flat = whole.reshape(n_exp, width * width).astype(jnp.float32)
    merged = jnp.dot(coeffs, flat, precision=HIGH).reshape(n_sys, width, width)
    merged_low = merged.astype(jnp.bfloat16)
    per_system = jnp.einsum("smi,smj->sij", inputs, masked, preferred_element_type=jnp.float32)
    term = jnp.einsum("se,sij->eij", coeffs, per_system, precision=HIGH)
    section = lax.psum_scatter(term, "dp", scatter_dimension=1, tiled=True)
    expert_grad = lax.psum_scatter(section, "fsdp", scatter_dimension=1, tiled=True)
    in_grad = jnp.einsum(
        "smj,sij->smi", masked, merged_low, preferred_element_type=jnp.float32
    ).astype(jnp.bfloat16)
    return (in_grad, expert_grad)


def solution(mesh):
    placed = (
        P(("dp", "fsdp"), None, None),
        P(("dp", "fsdp"), None, None),
        P(("dp", "fsdp"), None),
        P(("dp", "fsdp")),
        P(None, ("dp", "fsdp"), None),
    )
    return jax.shard_map(
        shards,
        mesh=mesh,
        in_specs=placed,
        out_specs=(P(("dp", "fsdp"), None, None), P(None, ("dp", "fsdp"), None)),
        check_vma=False,
    )
```

profile of v0, /device:TPU:0, one launch (start us, length us, event | category | flops | bytes accessed | tf_op | source)
XLA Modules:
  0.0 277.7 jit_solution(11128977890915783579)
XLA Ops:
  8.0 0.0 copy-start
  8.0 0.0 reduce-scatter.3.cloned.1.call-start
  8.1 0.8 iota_compare_fusion
  8.9 0.4 copy-done
  9.2 4.1 %fusion.7 = f32[4,512,512]{2,1,0:T(8,128)} fusion(bf16[4,256,512]{2,1,0:T(8,128)(2,1)S(1)} %copy-done, bf16[4,256,512]{2,1,0:T(8,128)(2,1)} %param.6, pred[4,256]{1,0:T(4,128)(4,1)S(1)} %iota_compare_fusion), kind=kOutput, calls=%fused_computation.9 | convolution fusion | flops 537395200 | bytes 6292480 | tf_op jit(solution)/shard_map/smi,smj->sij/dot_general | solution.py:19
  13.3 0.0 copy-start.2
  13.3 5.5 %copy.10 = f32[4,512,512]{1,0,2:T(4,128)} copy(f32[4,512,512]{2,1,0:T(8,128)} %fusion.7) | data formatting | bytes 8388608 | tf_op jit(solution)/shard_map/smi,smj->sij/dot_general | solution.py:19
  18.8 0.0 copy-done.2
  18.8 17.5 %fusion.3 = f32[16,512,512]{2,0,1:T(8,128)} fusion(f32[4,512,512]{1,0,2:T(4,128)} %copy.10, s32[4,16]{1,0:T(4,128)S(1)} %copy-done.2), kind=kOutput, calls=%fused_computation.3 | convolution fusion | flops 201326720 | bytes 20971776 | tf_op jit(solution)/shard_map/se,sij->eij/dot_general | solution.py:20
  36.3 0.0 reduce-scatter.3.cloned.1.call-update
  36.4 0.0 all-gather.2.cloned.1.call-start
  36.4 0.5 all-gather.2.cloned.1.call-update
  36.9 0.0 reduce-scatter.5.cloned.1.call-start
  37.0 209.4 %reduce-scatter.3.cloned.1.call-done = f32[16,32,512]{2,0,1:T(8,128)} async-done(((f32[16,512,512]{2,0,1:T(8,128)}), f32[16,32,512]{2,0,1:T(8,128)}) %reduce-scatter.3.cloned.1.call-update) | async-done | bytes 1048592 | tf_op jit(solution)/shard_map/reduce_scatter | solution.py:21
  246.4 0.0 reduce-scatter.5.cloned.1.call-update
  246.4 0.0 all-gather.2.cloned.1.call-done
  246.5 0.0 copy-start.1
  246.5 11.3 %fusion = bf16[4,512,512]{2,0,1:T(4,128)(2,1)S(1)} fusion(s32[4,16]{1,0:T(4,128)S(1)} %copy-done.2, bf16[2,8,512,512]{3,2,1,0:T(8,128)(2,1)} %bitcast.23), kind=kOutput, calls=%fused_computation | convolution fusion | flops 201326720 | bytes 10486016 | tf_op jit(solution)/shard_map/dot_general | solution.py:17
  257.7 0.0 copy-done.1
  257.8 2.0 fusion.6
  259.7 8.4 %reduce-scatter.5.cloned.1.call-done = f32[16,16,512]{2,0,1:T(8,128)} async-done(((f32[16,32,512]{2,0,1:T(8,128)}), f32[16,16,512]{2,0,1:T(8,128)}) %reduce-scatter.5.cloned.1.call-update) | async-done | bytes 524304 | tf_op jit(solution)/shard_map/reduce_scatter | solution.py:22
  268.2 2.1 copy.7
Async XLA Ops:
  8.0 1.2 copy-start
  8.0 238.4 %reduce-scatter.3.cloned.1.call-start = ((), (), s32[]{:S(2)}) async-start(), calls=%async_computation.3 | async-start | bytes 17825792 | tf_op jit(solution)/shard_map/reduce_scatter | solution.py:21
  13.3 5.5 %copy-start.2 = (s32[4,16]{1,0:T(4,128)S(1)}, s32[4,16]{1,0:T(4,128)}, u32[]{:S(2)}) copy-start(s32[4,16]{1,0:T(4,128)} %param.7) | copy-start | bytes 772
  36.4 210.1 %all-gather.2.cloned.1.call-start = ((), (), s32[]{:S(2)}) async-start(), calls=%async_computation.2 | async-start | bytes 8650752 | tf_op jit(solution)/shard_map/all_gather | solution.py:15
  36.9 231.2 %reduce-scatter.5.cloned.1.call-start = ((), (), s32[]{:S(2)}) async-start(), calls=%async_computation.4 | async-start | bytes 1572864 | tf_op jit(solution)/shard_map/reduce_scatter | solution.py:22
  246.5 11.3 %copy-start.1 = (bf16[4,256,512]{2,1,0:T(8,128)(2,1)S(1)}, bf16[4,256,512]{2,1,0:T(8,128)(2,1)}, u32[]{:S(2)}) copy-start(bf16[4,256,512]{2,1,0:T(8,128)(2,1)} %param.6) | copy-start | bytes 3145732
Sparse Core Ops, SparseCore 0:
  36.5 209.8 reduce-scatter.2
  248.6 19.4 reduce-scatter.4
Sparse Core Ops, SparseCore 1:
  39.9 134.2 all-gather.1
where the time goes:
time: 278 us
  waiting for transfers between devices  218 us (78%)
  matrix products  34.9 us (13%)
  between operations  15.5 us (6%)
  local copies, waits for them, and re-layouts  8 us (3%)
    reduce_scatter x1, waiting for transfers between devices, shards(): section = lax.psum_scatter(term, 'dp', scatter_dimension=1, tiled=True)  209 us
    dot_general x1, matrix products, shards(): term = jnp.einsum('se,sij->eij', coeffs, per_system, precision=HIGH)  17.5 us
    dot_general x1, matrix products, shards(): merged = jnp.dot(coeffs, flat, precision=HIGH).reshape(n_sys, width, width)  11.3 us
    reduce_scatter x1, waiting for transfers between devices, shards(): lax.psum_scatter(section, 'fsdp', scatter_dimension=1, tiled=True)  8.43 us
  transfers between devices with their start and end apart: 3, of which 2 were waited for; matrix products, arithmetic and copies ran while one was open for 5% of the time, Pallas kernels for 0%

commit v1 on v0

v1 whole, which is shorter than its diff:
```python
import functools

import jax
import jax.numpy as jnp
from jax import lax
from jax.experimental import pallas as pl
from jax.experimental.pallas import tpu as pltpu
from jax.sharding import PartitionSpec as P

HIGH = lax.Precision.HIGHEST
MESH = pl.DeviceIdType.MESH
BF16 = jnp.bfloat16
F32 = jnp.float32


def dot(a, b, ca, cb):
    return lax.dot_general(a, b, (((ca,), (cb,)), ((), ())), preferred_element_type=F32)


def kernel(nz, n_sys, n_exp, rows, width,
           counts_ref, in_ref, og_ref, ex_ref, kl_ref,
           ig_ref, eg_ref,
           mk, pb, g, eo, eb, er, zs, zr, xg, ka, kr, mb, mr,
           loc, ka_s, ka_r, kr_s, kr_r, xz_s, xz_r, xy_s, xy_r,
           pb_s, pb_r, eb_s, eb_r, zs_s, zs_r, mb_s, mb_r):
    dp = lax.axis_index("dp")
    y = lax.axis_index("fsdp")
    z = dp // 4
    x = lax.rem(dp // 2, 2)
    c = lax.rem(dp, 2)
    sr = n_sys * rows
    er_rows = n_exp * rows

    def flip(v, d):
        return lax.rem(v + d, 2)

    def at(zz, xx, cc, yy):
        return ((zz * 2 + xx) * 2 + cc, yy)

    def zto(k):
        return lax.rem(z + k, nz)

    def zfrom(k):
        return lax.rem(z + nz - k, nz)

    rest = (1, 2, 3)
    peers = [at(z, x, flip(c, 1), y)]
    peers += [at(z, flip(x, 1), flip(c, d), y) for d in (0, 1)]
    peers += [at(z, x, flip(c, d), flip(y, 1)) for d in (0, 1)]
    peers += [at(zto(k), x, c, y) for k in range(1, nz)]
    barrier = pltpu.get_barrier_semaphore()
    for peer in peers:
        pl.semaphore_signal(barrier, inc=1, device_id=peer, device_id_type=MESH)
    pl.semaphore_wait(barrier, len(peers))

    def send(src, dst, s, r, peer):
        copy = pltpu.make_async_remote_copy(
            src_ref=src, dst_ref=dst, send_sem=s, recv_sem=r, device_id=peer, device_id_type=MESH
        )
        copy.start()
        return copy

    n_loc = [0]

    def local(src, dst):
        copy = pltpu.make_async_copy(src, dst, loc.at[n_loc[0]])
        n_loc[0] += 1
        copy.start()
        return copy

    sent = []
    xc = x * 2 + c
    yc = y * 2 + c

    ka_c, kr_c, xz_c, xy_c = [], [], [], []
    for j in rest:
        ka_c.append(send(kl_ref, ka.at[xc], ka_s.at[j - 1], ka_r.at[j - 1],
                         at(z, flip(x, j // 2), flip(c, j % 2), y)))
        kr_c.append(send(kl_ref, kr.at[yc], kr_s.at[j - 1], kr_r.at[j - 1],
                         at(z, x, flip(c, j % 2), flip(y, j // 2))))
    ka_own = local(kl_ref, ka.at[xc])
    kr_own = local(kl_ref, kr.at[yc])
    for k in range(1, nz):
        xz_c.append(send(ex_ref, xg.at[y, z], xz_s.at[k], xz_r.at[k], at(zto(k), x, c, y)))
    xy_c.append(send(ex_ref, xg.at[y, z], xy_s.at[0], xy_r.at[0], at(z, x, c, flip(y, 1))))
    ex_own = local(ex_ref, xg.at[y, z])
    sent += ka_c + kr_c + xz_c + xy_c

    for s in range(n_sys):
        slot = lax.broadcasted_iota(jnp.int32, og_ref.shape[1:], 0)
        mk[s] = jnp.where(slot < counts_ref[s], og_ref[s], jnp.zeros(og_ref.shape[1:], BF16))
        prod = dot(in_ref[s], mk[s], 0, 0).astype(BF16)
        for b in range(width // rows):
            yy, cc, xx, zz = b % 2, b // 2 % 2, b // 4 % 2, b // 8
            pb[yy * 2 + cc, zz, xx, s * rows:(s + 1) * rows, :] = prod[b * rows:(b + 1) * rows, :]
    order = list(range(1, nz)) + [0]
    pb_c, g_own = {}, {}
    for k in order:
        for j in rest:
            yy, cc = flip(y, j // 2), flip(c, j % 2)
            pb_c[k, j] = send(pb.at[yy * 2 + cc, zto(k)], g.at[k, :, yc],
                              pb_s.at[k, j - 1], pb_r.at[k, j - 1], at(z, x, cc, yy))
        g_own[k] = local(pb.at[yc, zto(k)], g.at[k, :, yc])
    sent += list(pb_c.values())

    mb_c, m_own = {}, {}

    def merge(ky, k):
        yy = flip(y, ky)
        zz = zfrom(k)
        block = xg[yy, zz]
        high = ka[:, 0].reshape(4 * sr, er_rows)
        low = ka[:, 1].reshape(4 * sr, er_rows)
        mb[ky, k] = (dot(high, block, 1, 0) + dot(low, block, 1, 0)).astype(BF16).reshape(
            4, n_sys, rows, width)
        for j in rest:
            xx, cc = flip(x, j // 2), flip(c, j % 2)
            mb_c[ky, k, j] = send(mb.at[ky, k, xx * 2 + cc], mr.at[:, zz, xc, yy],
                                  mb_s.at[ky, k, j - 1], mb_r.at[ky, k, j - 1], at(z, xx, cc, y))
            sent.append(mb_c[ky, k, j])
        m_own[ky, k] = local(mb.at[ky, k, xc], mr.at[:, zz, xc, yy])

    def expert_term(k, xx):
        block = g[k, xx].reshape(4 * sr, width)
        high = kr[:, 0].reshape(4 * sr, er_rows)
        low = kr[:, 1].reshape(4 * sr, er_rows)
        return dot(high, block, 0, 0) + dot(low, block, 0, 0)

    ka_own.wait()
    kr_own.wait()
    ex_own.wait()
    for copy in ka_c + kr_c:
        copy.wait_recv()
    merge(0, 0)
    eb_c = {}
    for k in order:
        if k:
            xz_c[k - 1].wait_recv()
            xy_c.append(send(xg.at[y, zfrom(k)], xg.at[y, zfrom(k)], xy_s.at[k], xy_r.at[k],
                             at(z, x, c, flip(y, 1))))
            sent.append(xy_c[-1])
            merge(0, k)
        g_own[k].wait()
        for j in rest:
            pb_c[k, j].wait_recv()
        eb[k] = expert_term(k, flip(x, 1)).astype(BF16)
        eb_c[k] = send(eb.at[k], er.at[k], eb_s.at[k], eb_r.at[k], at(z, flip(x, 1), c, y))
        sent.append(eb_c[k])
        eo[k] = expert_term(k, x)
    zs_c = {}
    for n, k in enumerate(order):
        eb_c[k].wait_recv()
        total = eo[k] + er[k].astype(F32)
        if k:
            zs[k] = total.astype(BF16)
            zs_c[k] = send(zs.at[k], zr.at[k], zs_s.at[k], zs_r.at[k], at(zto(k), x, c, y))
            sent.append(zs_c[k])
        else:
            eo[0] = total
        xy_c[n].wait_recv()
        merge(1, n)
    for key in mb_c:
        mb_c[key].wait_recv()
    for key in m_own:
        m_own[key].wait()
    for s in range(n_sys):
        ig_ref[s] = dot(mk[s], mr[s].reshape(width, width), 1, 1).astype(BF16)
    total = eo[0]
    for k in range(1, nz):
        zs_c[k].wait_recv()
        total = total + zr[k].astype(F32)
    eg_ref[...] = total
    for copy in sent:
        copy.wait_send()


def fused(inputs, out_grad, coeff_fixed, atom_counts, experts, nz):
    n_sys, n_slots, width = inputs.shape
    n_exp, rows, _ = experts.shape
    sr, er_rows = n_sys * rows, n_exp * rows
    high = (coeff_fixed // 64).astype(F32) / 64.0
    low = (coeff_fixed % 64).astype(F32) / 4096.0
    halves = jnp.stack([high, low])
    eye = jnp.eye(rows, dtype=F32)
    kl = (halves[:, :, None, :, None] * eye[None, None, :, None, :]).reshape(2, sr, er_rows).astype(BF16)
    vmem = pl.BlockSpec(memory_space=pltpu.VMEM)
    dma = pltpu.SemaphoreType.DMA
    in_grad, expert_grad = pl.pallas_call(
        functools.partial(kernel, nz, n_sys, n_exp, rows, width),
        out_shape=(
            jax.ShapeDtypeStruct(inputs.shape, BF16),
            jax.ShapeDtypeStruct((er_rows, width), F32),
        ),
        in_specs=[pl.BlockSpec(memory_space=pltpu.SMEM)] + [vmem] * 4,
        out_specs=(vmem, vmem),
        scratch_shapes=[
            pltpu.VMEM(out_grad.shape, BF16),
            pltpu.VMEM((4, nz, 2, sr, width), BF16),
            pltpu.VMEM((nz, 2, 4, sr, width), BF16),
            pltpu.VMEM((nz, er_rows, width), F32),
            pltpu.VMEM((nz, er_rows, width), BF16),
            pltpu.VMEM((nz, er_rows, width), BF16),
            pltpu.VMEM((nz, er_rows, width), BF16),
            pltpu.VMEM((nz, er_rows, width), BF16),
            pltpu.VMEM((2, nz, er_rows, width), BF16),
            pltpu.VMEM((4, 2, sr, er_rows), BF16),
            pltpu.VMEM((4, 2, sr, er_rows), BF16),
            pltpu.VMEM((2, nz, 4, n_sys, rows, width), BF16),
            pltpu.VMEM((n_sys, nz, 4, 2, rows, width), BF16),
            dma((3 + 3 * nz,)),
            dma((3,)), dma((3,)), dma((3,)), dma((3,)),
            dma((nz,)), dma((nz,)), dma((nz,)), dma((nz,)),
            dma((nz, 3)), dma((nz, 3)), dma((nz,)), dma((nz,)),
            dma((nz,)), dma((nz,)), dma((2, nz, 3)), dma((2, nz, 3)),
        ],
        compiler_params=pltpu.CompilerParams(collective_id=0, has_side_effects=True),
    )(atom_counts, inputs, out_grad, experts.reshape(er_rows, width), kl)
    return in_grad, expert_grad.reshape(n_exp, rows, width)


def plain(inputs, out_grad, coeff_fixed, atom_counts, experts):
    both = ("dp", "fsdp")
    n_sys, n_slots, width = inputs.shape
    n_exp, rows, _ = experts.shape
    coeffs = lax.all_gather(coeff_fixed, both, axis=0, tiled=True).astype(F32) / 4096.0
    valid = lax.broadcasted_iota(jnp.int32, (n_sys, n_slots), 1) < atom_counts[:, None]
    masked = jnp.where(valid[:, :, None], out_grad, jnp.zeros_like(out_grad))
    merged = jnp.einsum("se,eij->sij", coeffs, experts.astype(F32), precision=HIGH).astype(BF16)
    merged = lax.all_to_all(merged, both, split_axis=0, concat_axis=1, tiled=True)
    per_system = jnp.einsum("smi,smj->sij", inputs, masked, preferred_element_type=F32)
    per_system = lax.all_to_all(per_system, both, split_axis=1, concat_axis=0, tiled=True)
    expert_grad = jnp.einsum("se,sij->eij", coeffs, per_system, precision=HIGH)
    in_grad = jnp.einsum("smj,sij->smi", masked, merged, preferred_element_type=F32).astype(BF16)
    return in_grad, expert_grad


def solution(mesh):
    n_dp, n_fsdp = mesh.shape["dp"], mesh.shape["fsdp"]

    def shards(inputs, out_grad, coeff_fixed, atom_counts, experts):
        if n_dp % 4 == 0 and n_fsdp == 2 and experts.shape[1] % 16 == 0 and inputs.shape[0] <= 4:
            return fused(inputs, out_grad, coeff_fixed, atom_counts, experts, n_dp // 4)
        return plain(inputs, out_grad, coeff_fixed, atom_counts, experts)

    placed = (
        P(("dp", "fsdp"), None, None),
        P(("dp", "fsdp"), None, None),
        P(("dp", "fsdp"), None),
        P(("dp", "fsdp")),
        P(None, ("dp", "fsdp"), None),
    )
    return jax.shard_map(
        shards,
        mesh=mesh,
        in_specs=placed,
        out_specs=(P(("dp", "fsdp"), None, None), P(None, ("dp", "fsdp"), None)),
        check_vma=False,
    )
```

time: 278 us -> 73.8 us (0.27)
  waiting for transfers between devices: 218 us -> 0 us
  Pallas kernels: 0 us -> 67.7 us
  matrix products: 34.9 us -> 0 us
  between operations: 15.5 us -> 0.67 us
  local copies, waits for them, and re-layouts: 8 us -> 3.97 us
    reduce_scatter x2 -> x0, waiting for transfers between devices: 218 us -> none  [the longest x1 209 us: shards(): section = lax.psum_scatter(term, 'dp', scatter_dimension=1, tiled=True)]
    pallas_call x0 -> x1, Pallas kernels: none -> 67.7 us  [fused(): pl.pallas_call(functools.partial(kernel, nz, n_sys, n_exp, rows, width),...]
    dot_general x4 -> x0, matrix products: 34.9 us -> none  [the longest x1 17.5 us: shards(): term = jnp.einsum('se,sij->eij', coeffs, per_system, precision=HIGH)]
    dot_general x1 -> x0, local copies, waits for them, and re-layouts: 5.46 us -> none  [shards(): jnp.einsum('smi,smj->sij', inputs, masked, preferred_element_type=jnp.flo...]
  transfers between devices with their start and end apart: 3 -> 0, of which waited for: 2 -> 0; matrix products, arithmetic and copies ran while one was open for 5% -> 0% of each run, Pallas kernels for 0% -> 0%
where the time goes in v1:
time: 73.8 us; the launch traced here: 73.6 us
  Pallas kernels  67.7 us (92%)
  local copies, waits for them, and re-layouts  3.97 us (5%)
  other arithmetic  1.35 us (2%)
    pallas_call x1, Pallas kernels, fused(): pl.pallas_call(functools.partial(kernel, nz, n_sys, n_exp, rows, width),...  67.7 us
    unnamed x4, local copies, waits for them, and re-layouts  3.12 us

profile of v1, /device:TPU:0, one launch (start us, length us, event | category | flops | bytes accessed | tf_op | source)
XLA Modules:
  0.0 73.6 jit_solution(9280357189114866241)
XLA Ops:
  0.6 0.7 fusion.3
  1.4 0.2 mul.23
  1.6 0.1 mul.20
  1.8 0.4 mul.21
  2.2 0.6 multiply_convert_fusion.kl_ref
  2.8 67.7 %shard_map.68 = (bf16[4,256,512]{2,1,0:T(8,128)(2,1)}, f32[256,512]{1,0:T(8,128)}) custom-call(s32[4]{0:T(128)} %counts_ref.1, bf16[4,256,512]{2,1,0:T(8,128)(2,1)} %in_ref.1, bf16[4,256,512]{2,1,0:T(8,128)(2,1)} %og_ref.1, bf16[256,512]{1,0:T(8,128)(2,1)} %bitcast.11, bf16[2,64,256]{2,1,0:T(8,128)(2,1)} %multiply_convert_fusion.kl_ref), custom_call_target="tpu_custom_call" | custom-call | tf_op jit(solution)/shard_map/pallas_call | solution.py:188
  70.5 0.0 copy-start
  70.5 2.3 %copy.9 = bf16[4,256,512]{2,1,0:T(8,128)(2,1)} copy(bf16[4,256,512]{2,1,0:T(8,128)(2,1)} %get-tuple-element.10) | data formatting | bytes 2097152
  72.8 0.0 copy-done
  72.8 0.8 %copy.10 = f32[16,16,512]{2,1,0:T(8,128)} copy(f32[16,16,512]{2,1,0:T(8,128)S(1)} %bitcast.10) | data formatting | bytes 1048576
  (3 shorter events, 0.0 us)
Async XLA Ops:
  70.5 2.3 %copy-start = (f32[256,512]{1,0:T(8,128)S(1)}, f32[256,512]{1,0:T(8,128)}, u32[]{:S(2)}) copy-start(f32[256,512]{1,0:T(8,128)} %get-tuple-element.5) | copy-start | bytes 1572868

commit v2 on v0

v2 whole, which is shorter than its diff:
```python
import functools

import jax
import jax.numpy as jnp
from jax import lax
from jax.experimental import pallas as pl
from jax.experimental.pallas import tpu as pltpu
from jax.sharding import PartitionSpec as P

HIGH = lax.Precision.HIGHEST
MESH = pl.DeviceIdType.MESH
BF16 = jnp.bfloat16
F32 = jnp.float32
NEAR_ORDER = (5, 7, 4, 1, 6, 3, 2)


def dot(a, b, ca, cb):
    return lax.dot_general(a, b, (((ca,), (cb,)), ((), ())), preferred_element_type=F32)


def kernel(nz, n_sys, n_exp, rows, width,
           counts_ref, co_ref, in_ref, og_ref, ex_ref,
           ig_ref, eg_ref,
           mk, kl, ka, kt, pb, g, eo, zs, zr, xg, mb, mr,
           loc, ka_s, ka_r, xz_s, xz_r, pb_s, pb_r, zs_s, zs_r, mb_s, mb_r):
    dp = lax.axis_index("dp")
    y = lax.axis_index("fsdp")
    z = dp // 4
    x = lax.rem(dp // 2, 2)
    c = lax.rem(dp, 2)
    me = x * 4 + c * 2 + y
    sr = n_sys * rows
    er_rows = n_exp * rows

    def flip(v, d):
        return lax.rem(v + d, 2)

    def near(j):
        xx, cc, yy = flip(x, j // 4), flip(c, j // 2 % 2), flip(y, j % 2)
        return xx * 4 + cc * 2 + yy, ((z * 2 + xx) * 2 + cc, yy)

    def along(k):
        return ((lax.rem(z + k, nz) * 2 + x) * 2 + c, y)

    def zto(k):
        return lax.rem(z + k, nz)

    def zfrom(k):
        return lax.rem(z + nz - k, nz)

    plane = NEAR_ORDER
    peers = [near(j)[1] for j in plane] + [along(k) for k in range(1, nz)]
    barrier = pltpu.get_barrier_semaphore()
    for peer in peers:
        pl.semaphore_signal(barrier, inc=1, device_id=peer, device_id_type=MESH)

    col = lax.broadcasted_iota(jnp.int32, (rows, er_rows), 1)
    row = lax.broadcasted_iota(jnp.int32, (rows, er_rows), 0)
    owner, diagonal = col // rows, col % rows == row
    for s in range(n_sys):
        spread = jnp.zeros((rows, er_rows), jnp.int32)
        for e in range(n_exp):
            spread = jnp.where(owner == e, co_ref[s, e], spread)
        spread = jnp.where(diagonal, spread, 0)
        high = (spread // 64).astype(F32) / 64.0
        low = (spread % 64).astype(F32) / 4096.0
        kl[0, s * rows:(s + 1) * rows, :] = high.astype(BF16)
        kl[1, s * rows:(s + 1) * rows, :] = low.astype(BF16)
    pl.semaphore_wait(barrier, len(peers))

    def send(src, dst, s, r, peer):
        copy = pltpu.make_async_remote_copy(
            src_ref=src, dst_ref=dst, send_sem=s, recv_sem=r, device_id=peer, device_id_type=MESH
        )
        copy.start()
        return copy

    n_loc = [0]

    def local(src, dst):
        copy = pltpu.make_async_copy(src, dst, loc.at[n_loc[0]])
        n_loc[0] += 1
        copy.start()
        return copy

    sent = []
    xz_c = {}
    for k in range(1, nz):
        xz_c[k] = send(ex_ref, xg.at[k], xz_s.at[k], xz_r.at[k], along(k))
    ka_c = [send(kl, ka.at[me], ka_s.at[j - 1], ka_r.at[j - 1], near(j)[1]) for j in plane]
    ka_own = local(kl, ka.at[me])
    sent += ka_c + list(xz_c.values())

    for s in range(n_sys):
        slot = lax.broadcasted_iota(jnp.int32, og_ref.shape[1:], 0)
        mk[s] = jnp.where(slot < counts_ref[s], og_ref[s], jnp.zeros(og_ref.shape[1:], BF16))
        prod = dot(in_ref[s], mk[s], 0, 0).astype(BF16)
        for b in range(width // rows):
            pb[b % 8, b // 8, s * rows:(s + 1) * rows, :] = prod[b * rows:(b + 1) * rows, :]
    order = list(range(1, nz)) + [0]
    pb_c, g_own = {}, {}
    for k in order:
        for j in plane:
            to, peer = near(j)
            pb_c[k, j] = send(pb.at[to, zto(k)], g.at[k, me], pb_s.at[k, j - 1], pb_r.at[k, j - 1], peer)
        g_own[k] = local(pb.at[me, zto(k)], g.at[k, me])
    sent += list(pb_c.values())

    mb_c, m_own = {}, {}

    def merge(k, block):
        zz = zfrom(k)
        high = ka[:, 0].reshape(8 * sr, er_rows)
        low = ka[:, 1].reshape(8 * sr, er_rows)
        mb[k] = (dot(high, block, 1, 0) + dot(low, block, 1, 0)).astype(BF16).reshape(
            8, n_sys, rows, width)
        for j in plane:
            to, peer = near(j)
            mb_c[k, j] = send(mb.at[k, to], mr.at[:, zz, me], mb_s.at[k, j - 1], mb_r.at[k, j - 1], peer)
            sent.append(mb_c[k, j])
        m_own[k] = local(mb.at[k, me], mr.at[:, zz, me])

    zs_c = {}

    def reduce(k):
        g_own[k].wait()
        for j in plane:
            pb_c[k, j].wait_recv()
        block = g[k].reshape(8 * sr, width)
        total = dot(kt[0], block, 1, 0) + dot(kt[1], block, 1, 0)
        if k:
            zs[k] = total.astype(BF16)
            zs_c[k] = send(zs.at[k], zr.at[k], zs_s.at[k], zs_r.at[k], along(k))
            sent.append(zs_c[k])
        else:
            eo[...] = total

    def finish(k):
        m_own[k].wait()
        for j in plane:
            mb_c[k, j].wait_recv()
        zz = zfrom(k)
        span = 8 * rows
        lanes = pl.ds(pl.multiple_of(zz * span, span), span)
        for s in range(n_sys):
            ig_ref[s, :, lanes] = dot(mk[s], mr[s, zz].reshape(span, width), 1, 1).astype(BF16)

    ka_own.wait()
    for copy in ka_c:
        copy.wait_recv()
    merge(0, ex_ref[...])
    kt[0] = ka[:, 0].reshape(8 * sr, er_rows).T
    kt[1] = ka[:, 1].reshape(8 * sr, er_rows).T
    for k in range(1, nz):
        reduce(k)
        xz_c[k].wait_recv()
        merge(k, xg[k])
    reduce(0)
    finish(0)
    for k in range(1, nz):
        zs_c[k].wait_recv()
        eo[...] += zr[k].astype(F32)
        if k < nz - 1:
            finish(k)
    eg_ref[...] = eo[...]
    finish(nz - 1)
    for copy in sent:
        copy.wait_send()


def fused(inputs, out_grad, coeff_fixed, atom_counts, experts, nz):
    n_sys, n_slots, width = inputs.shape
    n_exp, rows, _ = experts.shape
    sr, er_rows = n_sys * rows, n_exp * rows
    vmem = pl.BlockSpec(memory_space=pltpu.VMEM)
    smem = pl.BlockSpec(memory_space=pltpu.SMEM)
    dma = pltpu.SemaphoreType.DMA
    in_grad, expert_grad = pl.pallas_call(
        functools.partial(kernel, nz, n_sys, n_exp, rows, width),
        out_shape=(
            jax.ShapeDtypeStruct(inputs.shape, BF16),
            jax.ShapeDtypeStruct((er_rows, width), F32),
        ),
        in_specs=[smem, smem, vmem, vmem, vmem],
        out_specs=(vmem, vmem),
        scratch_shapes=[
            pltpu.VMEM(out_grad.shape, BF16),
            pltpu.VMEM((2, sr, er_rows), BF16),
            pltpu.VMEM((8, 2, sr, er_rows), BF16),
            pltpu.VMEM((2, er_rows, 8 * sr), BF16),
            pltpu.VMEM((8, nz, sr, width), BF16),
            pltpu.VMEM((nz, 8, sr, width), BF16),
            pltpu.VMEM((er_rows, width), F32),
            pltpu.VMEM((nz, er_rows, width), BF16),
            pltpu.VMEM((nz, er_rows, width), BF16),
            pltpu.VMEM((nz, er_rows, width), BF16),
            pltpu.VMEM((nz, 8, n_sys, rows, width), BF16),
            pltpu.VMEM((n_sys, nz, 8, rows, width), BF16),
            dma((1 + 2 * nz,)),
            dma((7,)), dma((7,)), dma((nz,)), dma((nz,)),
            dma((nz, 7)), dma((nz, 7)), dma((nz,)), dma((nz,)),
            dma((nz, 7)), dma((nz, 7)),
        ],
        compiler_params=pltpu.CompilerParams(collective_id=0, has_side_effects=True),
    )(atom_counts, coeff_fixed, inputs, out_grad, experts.reshape(er_rows, width))
    return in_grad, expert_grad.reshape(n_exp, rows, width)


def plain(inputs, out_grad, coeff_fixed, atom_counts, experts):
    both = ("dp", "fsdp")
    n_sys, n_slots, width = inputs.shape
    n_exp, rows, _ = experts.shape
    coeffs = lax.all_gather(coeff_fixed, both, axis=0, tiled=True).astype(F32) / 4096.0
    valid = lax.broadcasted_iota(jnp.int32, (n_sys, n_slots), 1) < atom_counts[:, None]
    masked = jnp.where(valid[:, :, None], out_grad, jnp.zeros_like(out_grad))
    merged = jnp.einsum("se,eij->sij", coeffs, experts.astype(F32), precision=HIGH).astype(BF16)
    merged = lax.all_to_all(merged, both, split_axis=0, concat_axis=1, tiled=True)
    per_system = jnp.einsum("smi,smj->sij", inputs, masked, preferred_element_type=F32)
    per_system = lax.all_to_all(per_system, both, split_axis=1, concat_axis=0, tiled=True)
    expert_grad = jnp.einsum("se,sij->eij", coeffs, per_system, precision=HIGH)
    in_grad = jnp.einsum("smj,sij->smi", masked, merged, preferred_element_type=F32).astype(BF16)
    return in_grad, expert_grad


def solution(mesh):
    n_dp, n_fsdp = mesh.shape["dp"], mesh.shape["fsdp"]

    def shards(inputs, out_grad, coeff_fixed, atom_counts, experts):
        if n_dp % 4 == 0 and n_fsdp == 2 and experts.shape[1] % 16 == 0 and inputs.shape[0] <= 4 and inputs.shape[2] % 128 == 0:
            return fused(inputs, out_grad, coeff_fixed, atom_counts, experts, n_dp // 4)
        return plain(inputs, out_grad, coeff_fixed, atom_counts, experts)

    placed = (
        P(("dp", "fsdp"), None, None),
        P(("dp", "fsdp"), None, None),
        P(("dp", "fsdp"), None),
        P(("dp", "fsdp")),
        P(None, ("dp", "fsdp"), None),
    )
    return jax.shard_map(
        shards,
        mesh=mesh,
        in_specs=placed,
        out_specs=(P(("dp", "fsdp"), None, None), P(None, ("dp", "fsdp"), None)),
        check_vma=False,
    )
```

time: 278 us -> 65.6 us (0.24)
  waiting for transfers between devices: 218 us -> 0 us
  Pallas kernels: 0 us -> 61.6 us
  matrix products: 34.9 us -> 0 us
  between operations: 15.5 us -> 0.65 us
  local copies, waits for them, and re-layouts: 8 us -> 3.12 us
    reduce_scatter x2 -> x0, waiting for transfers between devices: 218 us -> none  [the longest x1 209 us: shards(): section = lax.psum_scatter(term, 'dp', scatter_dimension=1, tiled=True)]
    pallas_call x0 -> x1, Pallas kernels: none -> 61.6 us  [fused(): pl.pallas_call(functools.partial(kernel, nz, n_sys, n_exp, rows, width),...]
    dot_general x4 -> x0, matrix products: 34.9 us -> none  [the longest x1 17.5 us: shards(): term = jnp.einsum('se,sij->eij', coeffs, per_system, precision=HIGH)]
    dot_general x1 -> x0, local copies, waits for them, and re-layouts: 5.46 us -> none  [shards(): jnp.einsum('smi,smj->sij', inputs, masked, preferred_element_type=jnp.flo...]
  transfers between devices with their start and end apart: 3 -> 0, of which waited for: 2 -> 0; matrix products, arithmetic and copies ran while one was open for 5% -> 0% of each run, Pallas kernels for 0% -> 0%
where the time goes in v2:
time: 65.6 us; the launch traced here: 65.4 us
  Pallas kernels  61.6 us (94%)
  local copies, waits for them, and re-layouts  3.12 us (5%)
    pallas_call x1, Pallas kernels, fused(): pl.pallas_call(functools.partial(kernel, nz, n_sys, n_exp, rows, width),...  61.6 us
    unnamed x4, local copies, waits for them, and re-layouts  3.12 us

profile of v2, /device:TPU:0, one launch (start us, length us, event | category | flops | bytes accessed | tf_op | source)
XLA Modules:
  0.0 65.4 jit_solution(8107500633989215240)
XLA Ops:
  0.6 61.6 %shard_map.68 = (bf16[4,256,512]{2,1,0:T(8,128)(2,1)}, f32[256,512]{1,0:T(8,128)}) custom-call(s32[4]{0:T(128)} %counts_ref.1, s32[4,16]{1,0:T(4,128)} %co_ref.1, bf16[4,256,512]{2,1,0:T(8,128)(2,1)} %in_ref.1, bf16[4,256,512]{2,1,0:T(8,128)(2,1)} %og_ref.1, bf16[256,512]{1,0:T(8,128)(2,1)} %bitcast.3), custom_call_target="tpu_custom_call" | custom-call | tf_op jit(solution)/shard_map/pallas_call | solution.py:178
  62.3 0.0 copy-start
  62.3 2.3 %copy.9 = bf16[4,256,512]{2,1,0:T(8,128)(2,1)} copy(bf16[4,256,512]{2,1,0:T(8,128)(2,1)} %get-tuple-element.8) | data formatting | bytes 2097152
  64.6 0.0 copy-done
  64.6 0.8 %copy.10 = f32[16,16,512]{2,1,0:T(8,128)} copy(f32[16,16,512]{2,1,0:T(8,128)S(1)} %bitcast.2) | data formatting | bytes 1048576
Async XLA Ops:
  62.3 2.3 %copy-start = (f32[256,512]{1,0:T(8,128)S(1)}, f32[256,512]{1,0:T(8,128)}, u32[]{:S(2)}) copy-start(f32[256,512]{1,0:T(8,128)} %get-tuple-element.5) | copy-start | bytes 1572868

commit v3 on v2

--- a/solution.py
+++ b/solution.py
@@ -21,7 +21,7 @@
 def kernel(nz, n_sys, n_exp, rows, width,
            counts_ref, co_ref, in_ref, og_ref, ex_ref,
            ig_ref, eg_ref,
-           mk, kl, ka, kt, pb, g, eo, zs, zr, xg, mb, mr,
+           mk, cl, ca, ka, kt, pb, g, eo, zs, zr, xg, mb, mr,
            loc, ka_s, ka_r, xz_s, xz_r, pb_s, pb_r, zs_s, zs_r, mb_s, mb_r):
     dp = lax.axis_index("dp")
     y = lax.axis_index("fsdp")
@@ -39,33 +39,35 @@
         xx, cc, yy = flip(x, j // 4), flip(c, j // 2 % 2), flip(y, j % 2)
         return xx * 4 + cc * 2 + yy, ((z * 2 + xx) * 2 + cc, yy)
 
-    def along(k):
-        return ((lax.rem(z + k, nz) * 2 + x) * 2 + c, y)
-
-    def zto(k):
-        return lax.rem(z + k, nz)
-
-    def zfrom(k):
-        return lax.rem(z + nz - k, nz)
+    half = z // 2
+    zm = z + half * (3 - 2 * z)
+
+    def actual(v):
+        return v + half * (3 - 2 * v)
+
+    def line(v):
+        return (actual(v) * 2 + x) * 2 + c, y
+
+    def arrival(n):
+        return actual((zm, 1 - zm, 2, 3)[n])
+
+    def target(n):
+        return actual((3, 2, 1 - zm, zm)[n])
 
     plane = NEAR_ORDER
-    peers = [near(j)[1] for j in plane] + [along(k) for k in range(1, nz)]
+    peers = [near(j)[1] for j in plane] + [((lax.rem(z + k, nz) * 2 + x) * 2 + c, y) for k in range(1, nz)]
     barrier = pltpu.get_barrier_semaphore()
     for peer in peers:
         pl.semaphore_signal(barrier, inc=1, device_id=peer, device_id_type=MESH)
 
-    col = lax.broadcasted_iota(jnp.int32, (rows, er_rows), 1)
-    row = lax.broadcasted_iota(jnp.int32, (rows, er_rows), 0)
-    owner, diagonal = col // rows, col % rows == row
+    col = lax.broadcasted_iota(jnp.int32, cl.shape[1:], 1)
+    row = lax.broadcasted_iota(jnp.int32, cl.shape[1:], 0)
+    fixed = jnp.zeros(cl.shape[1:], jnp.int32)
     for s in range(n_sys):
-        spread = jnp.zeros((rows, er_rows), jnp.int32)
         for e in range(n_exp):
-            spread = jnp.where(owner == e, co_ref[s, e], spread)
-        spread = jnp.where(diagonal, spread, 0)
-        high = (spread // 64).astype(F32) / 64.0
-        low = (spread % 64).astype(F32) / 4096.0
-        kl[0, s * rows:(s + 1) * rows, :] = high.astype(BF16)
-        kl[1, s * rows:(s + 1) * rows, :] = low.astype(BF16)
+            fixed = jnp.where((row == s) & (col == e), co_ref[s, e], fixed)
+    cl[0] = ((fixed >> 6).astype(F32) / 64.0).astype(BF16)
+    cl[1] = ((fixed & 63).astype(F32) / 4096.0).astype(BF16)
     pl.semaphore_wait(barrier, len(peers))
 
     def send(src, dst, s, r, peer):
@@ -84,12 +86,21 @@
         return copy
 
     sent = []
-    xz_c = {}
-    for k in range(1, nz):
-        xz_c[k] = send(ex_ref, xg.at[k], xz_s.at[k], xz_r.at[k], along(k))
-    ka_c = [send(kl, ka.at[me], ka_s.at[j - 1], ka_r.at[j - 1], near(j)[1]) for j in plane]
-    ka_own = local(kl, ka.at[me])
-    sent += ka_c + list(xz_c.values())
+    ca_c = [send(cl, ca.at[me], ka_s.at[j - 1], ka_r.at[j - 1], near(j)[1]) for j in plane]
+    ca_own = local(cl, ca.at[me])
+
+    def relay(src, block, n, to):
+        return pltpu.make_async_remote_copy(
+            src_ref=src, dst_ref=xg.at[block], send_sem=xz_s.at[n], recv_sem=xz_r.at[block],
+            device_id=to, device_id_type=MESH)
+
+    relay(ex_ref, z, 0, line(1 - zm)).start()
+
+    @pl.when(zm == 1)
+    def _():
+        relay(ex_ref, z, nz, line(2)).start()
+
+    sent += ca_c
 
     for s in range(n_sys):
         slot = lax.broadcasted_iota(jnp.int32, og_ref.shape[1:], 0)
@@ -97,22 +108,20 @@
         prod = dot(in_ref[s], mk[s], 0, 0).astype(BF16)
         for b in range(width // rows):
             pb[b % 8, b // 8, s * rows:(s + 1) * rows, :] = prod[b * rows:(b + 1) * rows, :]
-    order = list(range(1, nz)) + [0]
+    order = list(range(nz))
     pb_c, g_own = {}, {}
     for k in order:
         for j in plane:
             to, peer = near(j)
-            pb_c[k, j] = send(pb.at[to, zto(k)], g.at[k, me], pb_s.at[k, j - 1], pb_r.at[k, j - 1], peer)
-        g_own[k] = local(pb.at[me, zto(k)], g.at[k, me])
+            pb_c[k, j] = send(pb.at[to, target(k)], g.at[k, me], pb_s.at[k, j - 1], pb_r.at[k, j - 1], peer)
+        g_own[k] = local(pb.at[me, target(k)], g.at[k, me])
     sent += list(pb_c.values())
 
     mb_c, m_own = {}, {}
 
     def merge(k, block):
-        zz = zfrom(k)
-        high = ka[:, 0].reshape(8 * sr, er_rows)
-        low = ka[:, 1].reshape(8 * sr, er_rows)
-        mb[k] = (dot(high, block, 1, 0) + dot(low, block, 1, 0)).astype(BF16).reshape(
+        zz = arrival(k)
+        mb[k] = (dot(ka[0], block, 1, 0) + dot(ka[1], block, 1, 0)).astype(BF16).reshape(
             8, n_sys, rows, width)
         for j in plane:
             to, peer = near(j)
@@ -122,48 +131,99 @@
 
     zs_c = {}
 
+    def landed(slot):
+        pltpu.make_async_remote_copy(
+            src_ref=zs.at[0], dst_ref=zr.at[slot], send_sem=zs_s.at[0], recv_sem=zs_r.at[slot],
+            device_id=line(1 - zm), device_id_type=MESH).wait_recv()
+        return zr[slot].astype(F32)
+
     def reduce(k):
         g_own[k].wait()
         for j in plane:
             pb_c[k, j].wait_recv()
         block = g[k].reshape(8 * sr, width)
-        total = dot(kt[0], block, 1, 0) + dot(kt[1], block, 1, 0)
-        if k:
-            zs[k] = total.astype(BF16)
-            zs_c[k] = send(zs.at[k], zr.at[k], zs_s.at[k], zs_r.at[k], along(k))
-            sent.append(zs_c[k])
-        else:
-            eo[...] = total
+        eo[k] = dot(kt[0], block, 1, 0) + dot(kt[1], block, 1, 0)
+
+    def forward(k):
+        @pl.when(zm == 1)
+        def _():
+            eo[k] += landed(k)
+
+        zs[k] = eo[k].astype(BF16)
+        slot = (2 * zm, 1 + 3 * zm, 3)[k]
+        zs_c[k] = send(zs.at[k], zr.at[slot], zs_s.at[k], zs_r.at[slot],
+                       line((zm + 1, zm + 1, 1 - zm)[k]))
+        sent.append(zs_c[k])
 
     def finish(k):
         m_own[k].wait()
         for j in plane:
             mb_c[k, j].wait_recv()
-        zz = zfrom(k)
+        zz = arrival(k)
         span = 8 * rows
         lanes = pl.ds(pl.multiple_of(zz * span, span), span)
         for s in range(n_sys):
             ig_ref[s, :, lanes] = dot(mk[s], mr[s, zz].reshape(span, width), 1, 1).astype(BF16)
 
-    ka_own.wait()
-    for copy in ka_c:
+    ca_own.wait()
+    for copy in ca_c:
         copy.wait_recv()
+    lane = lax.broadcasted_iota(jnp.int32, (cl.shape[2], er_rows), 1)
+    first = lax.broadcasted_iota(jnp.int32, (cl.shape[2], er_rows), 0) * rows
+    pick = jnp.where((lane >= first) & (lane < first + rows), 1.0, 0.0).astype(BF16)
+    wide = dot(ca[...].reshape(16 * cl.shape[1], cl.shape[2]), pick, 1, 0)
+    across = lax.broadcasted_iota(jnp.int32, (rows, er_rows), 1) % rows
+    diagonal = across == lax.broadcasted_iota(jnp.int32, (rows, er_rows), 0)
+    for p in range(8):
+        for h in range(2):
+            for s in range(n_sys):
+                at = (p * 2 + h) * cl.shape[1] + s
+                value = jnp.broadcast_to(wide[at:at + 1, :], (rows, er_rows))
+                spot = (p * n_sys + s) * rows
+                ka[h, spot:spot + rows, :] = jnp.where(diagonal, value, 0.0).astype(BF16)
     merge(0, ex_ref[...])
-    kt[0] = ka[:, 0].reshape(8 * sr, er_rows).T
-    kt[1] = ka[:, 1].reshape(8 * sr, er_rows).T
-    for k in range(1, nz):
-        reduce(k)
-        xz_c[k].wait_recv()
-        merge(k, xg[k])
+    kt[0] = ka[0].T
+    kt[1] = ka[1].T
+
+    def arrived(n):
+        block = arrival(n)
+        copy = relay(ex_ref, block, n, line(1 - zm))
+        copy.wait_recv()
+
+        @pl.when(zm == 1)
+        def _():
+            relay(xg.at[block], block, n, line(2 if n == 1 else 0)).start()
+
+        merge(n, xg[block])
+
+    arrived(1)
     reduce(0)
+    forward(0)
+    arrived(2)
+    reduce(1)
+    forward(1)
+    arrived(3)
+    reduce(2)
+    forward(2)
+    reduce(3)
     finish(0)
-    for k in range(1, nz):
-        zs_c[k].wait_recv()
-        eo[...] += zr[k].astype(F32)
-        if k < nz - 1:
-            finish(k)
-    eg_ref[...] = eo[...]
-    finish(nz - 1)
+    finish(1)
+    finish(2)
+    eg_ref[...] = eo[3] + landed(3)
+
+    @pl.when(zm == 1)
+    def _():
+        eg_ref[...] += landed(4)
+
+    finish(3)
+    relay(ex_ref, z, 0, line(1 - zm)).wait_send()
+
+    @pl.when(zm == 1)
+    def _():
+        relay(ex_ref, z, nz, line(2)).wait_send()
+        for n in range(1, nz):
+            relay(ex_ref, z, n, line(0)).wait_send()
+
     for copy in sent:
         copy.wait_send()
 
@@ -185,20 +245,21 @@
         out_specs=(vmem, vmem),
         scratch_shapes=[
             pltpu.VMEM(out_grad.shape, BF16),
-            pltpu.VMEM((2, sr, er_rows), BF16),
-            pltpu.VMEM((8, 2, sr, er_rows), BF16),
+            pltpu.VMEM((2, 16, 128), BF16),
+            pltpu.VMEM((8, 2, 16, 128), BF16),
+            pltpu.VMEM((2, 8 * sr, er_rows), BF16),
             pltpu.VMEM((2, er_rows, 8 * sr), BF16),
             pltpu.VMEM((8, nz, sr, width), BF16),
             pltpu.VMEM((nz, 8, sr, width), BF16),
-            pltpu.VMEM((er_rows, width), F32),
-            pltpu.VMEM((nz, er_rows, width), BF16),
-            pltpu.VMEM((nz, er_rows, width), BF16),
+            pltpu.VMEM((nz, er_rows, width), F32),
+            pltpu.VMEM((nz - 1, er_rows, width), BF16),
+            pltpu.VMEM((nz + 1, er_rows, width), BF16),
             pltpu.VMEM((nz, er_rows, width), BF16),
             pltpu.VMEM((nz, 8, n_sys, rows, width), BF16),
             pltpu.VMEM((n_sys, nz, 8, rows, width), BF16),
             dma((1 + 2 * nz,)),
-            dma((7,)), dma((7,)), dma((nz,)), dma((nz,)),
-            dma((nz, 7)), dma((nz, 7)), dma((nz,)), dma((nz,)),
+            dma((7,)), dma((7,)), dma((nz + 1,)), dma((nz,)),
+            dma((nz, 7)), dma((nz, 7)), dma((nz - 1,)), dma((nz + 1,)),
             dma((nz, 7)), dma((nz, 7)),
         ],
         compiler_params=pltpu.CompilerParams(collective_id=0, has_side_effects=True),
@@ -226,7 +287,9 @@
     n_dp, n_fsdp = mesh.shape["dp"], mesh.shape["fsdp"]
 
     def shards(inputs, out_grad, coeff_fixed, atom_counts, experts):
-        if n_dp % 4 == 0 and n_fsdp == 2 and experts.shape[1] % 16 == 0 and inputs.shape[0] <= 4 and inputs.shape[2] % 128 == 0:
+        n_sys, _, width = inputs.shape
+        n_exp, rows, _ = experts.shape
+        if n_dp == 16 and n_fsdp == 2 and rows % 16 == 0 and n_sys <= 16 and n_exp <= 128:
             return fused(inputs, out_grad, coeff_fixed, atom_counts, experts, n_dp // 4)
         return plain(inputs, out_grad, coeff_fixed, atom_counts, experts)
 

time: 65.6 us -> 61.9 us (0.944)
  Pallas kernels: 61.6 us -> 57.9 us
    pallas_call x1, Pallas kernels: 61.6 us -> 57.9 us  [fused(): pl.pallas_call(functools.partial(kernel, nz, n_sys, n_exp, rows, width),...]
where the time goes in v3:
time: 61.9 us; the launch traced here: 61.7 us
  Pallas kernels  57.9 us (94%)
  local copies, waits for them, and re-layouts  3.12 us (5%)
  between operations  0.65 us (1%)
    pallas_call x1, Pallas kernels, fused(): pl.pallas_call(functools.partial(kernel, nz, n_sys, n_exp, rows, width),...  57.9 us
    unnamed x4, local copies, waits for them, and re-layouts  3.12 us

profile of v3, /device:TPU:0, one launch (start us, length us, event | category | flops | bytes accessed | tf_op | source)
XLA Modules:
  0.0 61.7 jit_solution(13847212791933792223)
XLA Ops:
  0.6 57.9 %shard_map.68 = (bf16[4,256,512]{2,1,0:T(8,128)(2,1)}, f32[256,512]{1,0:T(8,128)}) custom-call(s32[4]{0:T(128)} %counts_ref.1, s32[4,16]{1,0:T(4,128)} %co_ref.1, bf16[4,256,512]{2,1,0:T(8,128)(2,1)} %in_ref.1, bf16[4,256,512]{2,1,0:T(8,128)(2,1)} %og_ref.1, bf16[256,512]{1,0:T(8,128)(2,1)} %bitcast.3), custom_call_target="tpu_custom_call" | custom-call | tf_op jit(solution)/shard_map/pallas_call | solution.py:238
  58.5 0.0 copy-start
  58.6 2.3 %copy.9 = bf16[4,256,512]{2,1,0:T(8,128)(2,1)} copy(bf16[4,256,512]{2,1,0:T(8,128)(2,1)} %get-tuple-element.8) | data formatting | bytes 2097152
  60.9 0.0 copy-done
  60.9 0.8 %copy.10 = f32[16,16,512]{2,1,0:T(8,128)} copy(f32[16,16,512]{2,1,0:T(8,128)S(1)} %bitcast.2) | data formatting | bytes 1048576
Async XLA Ops:
  58.5 2.3 %copy-start = (f32[256,512]{1,0:T(8,128)S(1)}, f32[256,512]{1,0:T(8,128)}, u32[]{:S(2)}) copy-start(f32[256,512]{1,0:T(8,128)} %get-tuple-element.5) | copy-start | bytes 1572868

commit v4 on v3

--- a/solution.py
+++ b/solution.py
@@ -105,16 +105,18 @@
     for s in range(n_sys):
         slot = lax.broadcasted_iota(jnp.int32, og_ref.shape[1:], 0)
         mk[s] = jnp.where(slot < counts_ref[s], og_ref[s], jnp.zeros(og_ref.shape[1:], BF16))
-        prod = dot(in_ref[s], mk[s], 0, 0).astype(BF16)
-        for b in range(width // rows):
-            pb[b % 8, b // 8, s * rows:(s + 1) * rows, :] = prod[b * rows:(b + 1) * rows, :]
-    order = list(range(nz))
     pb_c, g_own = {}, {}
-    for k in order:
+    for k in range(nz):
+        span = 8 * rows
+        lanes = pl.ds(pl.multiple_of(target(k) * span, span), span)
+        for s in range(n_sys):
+            prod = dot(in_ref[s, :, lanes], mk[s], 0, 0).astype(BF16)
+            for b in range(8):
+                pb[b, k, s * rows:(s + 1) * rows, :] = prod[b * rows:(b + 1) * rows, :]
         for j in plane:
             to, peer = near(j)
-            pb_c[k, j] = send(pb.at[to, target(k)], g.at[k, me], pb_s.at[k, j - 1], pb_r.at[k, j - 1], peer)
-        g_own[k] = local(pb.at[me, target(k)], g.at[k, me])
+            pb_c[k, j] = send(pb.at[to, k], g.at[k, me], pb_s.at[k, j - 1], pb_r.at[k, j - 1], peer)
+        g_own[k] = local(pb.at[me, k], g.at[k, me])
     sent += list(pb_c.values())
 
     mb_c, m_own = {}, {}
@@ -129,8 +131,6 @@
             sent.append(mb_c[k, j])
         m_own[k] = local(mb.at[k, me], mr.at[:, zz, me])
 
-    zs_c = {}
-
     def landed(slot):
         pltpu.make_async_remote_copy(
             src_ref=zs.at[0], dst_ref=zr.at[slot], send_sem=zs_s.at[0], recv_sem=zs_r.at[slot],
@@ -144,16 +144,23 @@
         block = g[k].reshape(8 * sr, width)
         eo[k] = dot(kt[0], block, 1, 0) + dot(kt[1], block, 1, 0)
 
-    def forward(k):
+    def onward(k):
+        slot = (2 * zm, 1 + 3 * zm, 3)[k]
+        return pltpu.make_async_remote_copy(
+            src_ref=zs.at[k], dst_ref=zr.at[slot], send_sem=zs_s.at[k], recv_sem=zs_r.at[slot],
+            device_id=line((zm + 1, zm + 1, 1 - zm)[k]), device_id_type=MESH)
+
+    def begin(k):
+        @pl.when(zm == 0)
+        def _():
+            zs[k] = eo[k].astype(BF16)
+            onward(k).start()
+
+    def proceed(k):
         @pl.when(zm == 1)
         def _():
-            eo[k] += landed(k)
-
-        zs[k] = eo[k].astype(BF16)
-        slot = (2 * zm, 1 + 3 * zm, 3)[k]
-        zs_c[k] = send(zs.at[k], zr.at[slot], zs_s.at[k], zs_r.at[slot],
-                       line((zm + 1, zm + 1, 1 - zm)[k]))
-        sent.append(zs_c[k])
+            zs[k] = (eo[k] + landed(k)).astype(BF16)
+            onward(k).start()
 
     def finish(k):
         m_own[k].wait()
@@ -194,17 +201,21 @@
         def _():
             relay(xg.at[block], block, n, line(2 if n == 1 else 0)).start()
 
-        merge(n, xg[block])
-
     arrived(1)
     reduce(0)
-    forward(0)
+    begin(0)
     arrived(2)
+    merge(1, xg[arrival(1)])
     reduce(1)
-    forward(1)
+    begin(1)
+    merge(2, xg[arrival(2)])
     arrived(3)
+    proceed(0)
+    merge(3, xg[arrival(3)])
+    proceed(1)
     reduce(2)
-    forward(2)
+    begin(2)
+    proceed(2)
     reduce(3)
     finish(0)
     finish(1)
@@ -217,6 +228,8 @@
 
     finish(3)
     relay(ex_ref, z, 0, line(1 - zm)).wait_send()
+    for k in range(nz - 1):
+        onward(k).wait_send()
 
     @pl.when(zm == 1)
     def _():

time: 61.9 us -> 60.9 us (0.984)
  Pallas kernels: 57.9 us -> 56.9 us
    pallas_call x1, Pallas kernels: 57.9 us -> 56.9 us  [fused(): pl.pallas_call(functools.partial(kernel, nz, n_sys, n_exp, rows, width),...]
where the time goes in v4:
time: 60.9 us; the launch traced here: 60.7 us
  Pallas kernels  56.9 us (93%)
  local copies, waits for them, and re-layouts  3.12 us (5%)
  between operations  0.65 us (1%)
    pallas_call x1, Pallas kernels, fused(): pl.pallas_call(functools.partial(kernel, nz, n_sys, n_exp, rows, width),...  56.9 us
    unnamed x4, local copies, waits for them, and re-layouts  3.12 us

profile of v4, /device:TPU:0, one launch (start us, length us, event | category | flops | bytes accessed | tf_op | source)
XLA Modules:
  0.0 60.7 jit_solution(7311973009183496785)
XLA Ops:
  0.6 56.9 %shard_map.68 = (bf16[4,256,512]{2,1,0:T(8,128)(2,1)}, f32[256,512]{1,0:T(8,128)}) custom-call(s32[4]{0:T(128)} %counts_ref.1, s32[4,16]{1,0:T(4,128)} %co_ref.1, bf16[4,256,512]{2,1,0:T(8,128)(2,1)} %in_ref.1, bf16[4,256,512]{2,1,0:T(8,128)(2,1)} %og_ref.1, bf16[256,512]{1,0:T(8,128)(2,1)} %bitcast.3), custom_call_target="tpu_custom_call" | custom-call | tf_op jit(solution)/shard_map/pallas_call | solution.py:251
  57.6 0.0 copy-start
  57.6 2.3 %copy.9 = bf16[4,256,512]{2,1,0:T(8,128)(2,1)} copy(bf16[4,256,512]{2,1,0:T(8,128)(2,1)} %get-tuple-element.8) | data formatting | bytes 2097152
  59.9 0.0 copy-done
  59.9 0.8 %copy.10 = f32[16,16,512]{2,1,0:T(8,128)} copy(f32[16,16,512]{2,1,0:T(8,128)S(1)} %bitcast.2) | data formatting | bytes 1048576
Async XLA Ops:
  57.6 2.3 %copy-start = (f32[256,512]{1,0:T(8,128)S(1)}, f32[256,512]{1,0:T(8,128)}, u32[]{:S(2)}) copy-start(f32[256,512]{1,0:T(8,128)} %get-tuple-element.5) | copy-start | bytes 1572868
